TPU v7x, 512 devices: a whole 4x8x8 slice. The times are simulated.
512 devices in a mesh: seq: 16 (over y_lo, x, core), head: 32 (over z, y_hi).
Axes of the slice: x: 4, y: 8 (y_hi: 4, y_lo: 2; y = y_hi * 2 + y_lo), z: 8, core: 2. Of those that a mesh axis runs over, the one named last changes fastest.
Arguments:
- queries: bfloat16 [2048, 8192], P('seq', 'head'), may hold values from -256 to 256
- key_rows: bfloat16 [2048, 128], P('seq'), may hold values from -6 to 6
- value_rows: bfloat16 [2048, 128], P('seq'), may hold values from -6 to 6
- pair_keys: bfloat16 [2048, 128], P('seq'), may hold values from 0.27 to 1.73
- pair_values: bfloat16 [2048, 128], P('seq'), may hold values from 0.099609375 to 1.8984375
- first_key: int32 [2048], P('seq'), may hold values from 0 to 2047, as said below
- residual: float32 [2048, 8192], P(('seq', 'head')), may hold values from -6 to 6
- out_weight: bfloat16 [8192, 8192], P('head', 'seq'), may hold values from -0.25 to 0.25
Outputs:
- updated: float32 [2048, 8192], P(('seq', 'head'))
Inputs may be any that keep to these rules, and one draw needn't show every extreme that they name: first_key never falls along the tokens, first_key[i] <= i, and first_key[i] = i where a document begins; positions 0 and 2047 begin one.
All inputs are finite; a program needn't handle non-finite values.
Results may differ from a plain program's by a relative error of at most 0.005.
Values may be sent and summed in bfloat16 or wider, within the bound.
A program may use at most 64 MiB of HBM per device.

v0:
```python
import math

import jax
import jax.numpy as jnp
from jax import lax
from jax.sharding import PartitionSpec as P

DH = 128
W1 = 512
W2 = 32


MASKED_SCORE = -1e30


def shifted(value, axis, steps):
    count = lax.axis_size(axis)
    leading, last = (max(0, -steps), min(count, count - steps))
    return lax.ppermute(value, axis, [(source, source + steps) for source in range(leading, last)])


def local(queries, key_rows, value_rows, pair_keys, pair_values, first_key, residual, out_weight):
    tok_local = queries.shape[0]
    head_local = queries.shape[1] // DH
    group_rows = math.gcd(64, tok_local)
    scale_factor = 1.0 / math.sqrt(DH)
    seq_base = lax.axis_index("seq") * tok_local
    reach_count = (W1 + tok_local - 1) // tok_local
    pieces = []
    for offset in range(reach_count, 0, -1):
        pieces.append(shifted((key_rows, value_rows), "seq", offset))
    halo_keys = jnp.concatenate([item[0] for item in pieces], axis=0)
    halo_values = jnp.concatenate([item[1] for item in pieces], axis=0)
    key_context = jnp.concatenate([halo_keys, key_rows], axis=0)
    value_context = jnp.concatenate([halo_values, value_rows], axis=0)
    pair_rim = shifted((pair_keys[tok_local - W2 :], pair_values[tok_local - W2 :]), "seq", 1)
    pair_key_context = jnp.concatenate([pair_rim[0], pair_keys], axis=0)
    pair_value_context = jnp.concatenate([pair_rim[1], pair_values], axis=0)
    context_len = W1 + tok_local
    key_span = min((W1 + group_rows + 127) // 128 * 128, context_len)
    query_heads = queries.reshape(tok_local, head_local, DH)

    def attend(row_start):
        query_blk = lax.dynamic_slice_in_dim(query_heads, row_start, group_rows, 0).astype(
            jnp.float32
        )
        pair_kspan = lax.dynamic_slice_in_dim(
            pair_key_context, row_start + 1, group_rows + W2 - 1, 0
        )
        pair_vspan = lax.dynamic_slice_in_dim(
            pair_value_context, row_start + 1, group_rows + W2 - 1, 0
        )
        pair_kwin = jnp.stack(
            [pair_kspan[index : index + W2] for index in range(group_rows)], axis=0
        )
        pair_vwin = jnp.stack(
            [pair_vspan[index : index + W2] for index in range(group_rows)], axis=0
        )
        pair_mix = (query_blk[:, :, None, :] * pair_kwin.astype(jnp.float32)[:, None, :, :]).astype(
            jnp.bfloat16
        )
        slice_start = jnp.minimum(row_start, context_len - key_span)
        logits = (
            jnp.einsum("ahod,kd->ahok", pair_mix, key_context, preferred_element_type=jnp.float32)
            * scale_factor
        )
        query_pos = seq_base + row_start + jnp.arange(group_rows, dtype=jnp.int32)
        key_pos = seq_base - W1 + slice_start + jnp.arange(key_span, dtype=jnp.int32)
        pair_pos = query_pos[:, None] - W2 + 1 + jnp.arange(W2, dtype=jnp.int32)[None, :]
        lower_bound = lax.dynamic_slice_in_dim(first_key, row_start, group_rows, 0)
        key_ok = (
            (key_pos[None, :] <= query_pos[:, None])
            & (key_pos[None, :] > query_pos[:, None] - W1)
            & (key_pos[None, :] >= lower_bound[:, None])
        )
        pair_ok = pair_pos >= lower_bound[:, None]
        allowed = key_ok[:, None, None, :] & pair_ok[:, None, :, None]
        logits = jnp.where(allowed, logits, MASKED_SCORE)
        row_top = jnp.max(logits, axis=(2, 3), keepdims=True)
        expo = jnp.where(allowed, jnp.exp(logits - row_top), 0.0)
        row_total = jnp.sum(expo, axis=(2, 3), keepdims=True)
        rounded_weight = (expo / row_total).astype(jnp.bfloat16)
        carried = jnp.einsum(
            "ahok,kd->ahod", rounded_weight, value_context, preferred_element_type=jnp.float32
        )
        return jnp.sum(carried * pair_vwin.astype(jnp.float32)[:, None, :, :], axis=2).astype(
            jnp.bfloat16
        )

    starts = jnp.arange(tok_local // group_rows, dtype=jnp.int32) * group_rows
    features = lax.map(attend, starts).reshape(tok_local, head_local * DH)
    partial_rows = jnp.dot(
        features,
        lax.all_gather(out_weight, "seq", axis=1, tiled=True),
        preferred_element_type=jnp.float32,
    )
    summed = lax.psum_scatter(partial_rows, "head", scatter_dimension=0, tiled=True)
    return residual + summed


def solution(mesh):
    placed = (
        P("seq", "head"),
        P("seq", None),
        P("seq", None),
        P("seq", None),
        P("seq", None),
        P("seq"),
        P(("seq", "head"), None),
        P("head", "seq"),
    )
    return jax.shard_map(
        local, mesh=mesh, in_specs=placed, out_specs=P(("seq", "head"), None), check_vma=False
    )
```

profile of v0, /device:TPU:14, one launch (start us, length us, event | category | flops | bytes accessed | tf_op | source)
XLA Modules:
  0.0 454.8 jit_solution(5699278378077924754)
XLA Ops:
  6.5 1.3 collective-permute-start.1
  7.8 1.3 collective-permute-start.2
  9.1 1.3 collective-permute-start.3
  10.4 1.9 collective-permute-start.4
  12.4 0.7 slice.1286
  13.1 1.9 collective-permute-start
  15.0 0.0 all-reduce.3.cloned.1.call-start
  15.1 0.7 slice.1287
  15.8 0.9 reshape.2082
  16.6 1.4 collective-permute-done
  18.1 1.9 collective-permute-start.9
  20.0 0.8 pad_maximum_fusion
  20.8 2.3 collective-permute-done.9
  23.0 1.3 collective-permute-start.5
  24.3 0.8 pad_maximum_fusion.1
  25.1 1.3 collective-permute-start.6
  26.4 1.3 collective-permute-start.7
  27.7 1.9 collective-permute-start.8
  29.7 0.8 constant_dynamic-update-slice_fusion.129
  30.5 2.1 collective-permute-done.5
  32.6 0.1 collective-permute-done.6
  32.7 1.4 collective-permute-done.7
  34.2 0.8 constant_dynamic-update-slice_fusion.134
  34.9 41.7 %while.15 = (s32[]{:T(128)}, bf16[2,64,2,128]{3,2,1,0:T(2,128)(2,1)S(1)}, s32[2]{0:T(128)S(1)}, s32[]{:T(128)}, s32[]{:T(128)}, /*index=5*/s32[128]{0:T(128)}, b...) while((s32[]{:T(128)}, ...), condition=%wide.region_4.5_spmd, body=%wide.region_0.4_spmd.sunk | while | flops 1383019264 | bytes 44728332 | solution.py:91
  34.9 0.6 dynamic_slice.58
  40.2 0.1 convert_element_type.96
  42.1 0.7 dynamic_slice.59
  44.0 0.1 compare_and_fusion.2
  44.1 0.1 add_compare_fusion.2
  44.2 0.9 broadcast_and_fusion.2
  45.1 2.5 fusion.150
  47.6 3.8 fusion.151
  51.4 0.1 convert_element_type.97
  51.6 4.2 multiply_reduce_fusion.2
  55.8 0.6 dynamic_slice.58
  61.1 0.1 convert_element_type.96
  62.9 0.7 dynamic_slice.59
  64.9 0.1 compare_and_fusion.2
  65.0 0.1 add_compare_fusion.2
  65.1 0.9 broadcast_and_fusion.2
  66.0 2.5 fusion.150
  68.5 3.8 fusion.151
  72.3 0.1 convert_element_type.97
  72.4 4.2 multiply_reduce_fusion.2
  76.7 4.9 %fusion.140 = f32[128,8192]{1,0:T(8,128)} fusion(bf16[256,8192]{1,0:T(8,128)(2,1)} %all-gather.2.cloned.1.call-done, bf16[16,8,2,128]{3,2,1,0:T(2,128)(2,1)S(1)} %bitcast.796), kind=kOutput, calls=%fused_computation.411 | convolution fusion | flops 536870912 | bytes 8454144 | tf_op jit(solution)/shard_map/dot_general | solution.py:92
  81.6 1.3 dynamic-slice
  83.5 362.8 %all-reduce.3.cloned.1.call-done = f32[128,8192]{1,0:T(8,128)} async-done(((f32[128,8192]{1,0:T(8,128)}), f32[128,8192]{1,0:T(8,128)}) %all-reduce.3.cloned.1.call-update) | async-done | bytes 4194320
  446.4 1.6 dynamic-slice_add_fusion
  (285 shorter events, 7.1 us)
Async XLA Ops:
  6.5 70.1 %all-gather.2.cloned.1.call-start = ((), (), s32[]{:S(2)}) async-start(), calls=%async_computation | async-start | bytes 4456448 | tf_op jit(solution)/shard_map/all_gather | solution.py:94
  6.5 18.6 %collective-permute-start.1 = (bf16[128,128]{1,0:T(8,128)(2,1)}, bf16[128,128]{1,0:T(8,128)(2,1)S(1)}, u32[]{:S(2)}, u32[]{:S(2)}) collective-permute-start(bf16[128,128]{1,0:T(8,128)(2,1)} %param.11), channel_id=1, source_target_pairs={{0,128},{32,160},{64,192},{96,224},{128,256},{160,288},{192,320},{... | collective-permute-start | bytes 98312 | tf_op jit(solution)/shard_map/ppermute | solution.py:19
  7.8 18.6 %collective-permute-start.2 = (bf16[128,128]{1,0:T(8,128)(2,1)}, bf16[128,128]{1,0:T(8,128)(2,1)S(1)}, u32[]{:S(2)}, u32[]{:S(2)}) collective-permute-start(bf16[128,128]{1,0:T(8,128)(2,1)} %param.11), channel_id=1, source_target_pairs={{0,96},{32,128},{64,160},{96,192},{128,224},{160,256},{192,288},{2... | collective-permute-start | bytes 98312 | tf_op jit(solution)/shard_map/ppermute | solution.py:19
  9.1 18.6 %collective-permute-start.3 = (bf16[128,128]{1,0:T(8,128)(2,1)}, bf16[128,128]{1,0:T(8,128)(2,1)S(1)}, u32[]{:S(2)}, u32[]{:S(2)}) collective-permute-start(bf16[128,128]{1,0:T(8,128)(2,1)} %param.11), channel_id=1, source_target_pairs={{0,64},{32,96},{64,128},{96,160},{128,192},{160,224},{192,256},{22... | collective-permute-start | bytes 98312 | tf_op jit(solution)/shard_map/ppermute | solution.py:19
  10.4 19.3 %collective-permute-start.4 = (bf16[128,128]{1,0:T(8,128)(2,1)}, bf16[128,128]{1,0:T(8,128)(2,1)S(1)}, u32[]{:S(2)}, u32[]{:S(2)}) collective-permute-start(bf16[128,128]{1,0:T(8,128)(2,1)} %param.11), channel_id=1, source_target_pairs={{0,32},{32,64},{64,96},{96,128},{128,160},{160,192},{192,224},{224... | collective-permute-start | bytes 98312 | tf_op jit(solution)/shard_map/ppermute | solution.py:19
  13.1 5.0 %collective-permute-start = (bf16[32,128]{1,0:T(8,128)(2,1)S(1)}, bf16[32,128]{1,0:T(8,128)(2,1)S(1)}, u32[]{:S(2)}, u32[]{:S(2)}) collective-permute-start(bf16[32,128]{1,0:T(8,128)(2,1)S(1)} %slice.1286), channel_id=1, source_target_pairs={{0,32},{32,64},{64,96},{96,128},{128,160},{160,192},{192,224},{224... | collective-permute-start | bytes 24584 | tf_op jit(solution)/shard_map/ppermute | solution.py:19
  15.0 431.4 %all-reduce.3.cloned.1.call-start = ((), (), s32[]{:S(2)}) async-start(), calls=%async_computation.1 | async-start | bytes 8388608
  18.1 5.0 %collective-permute-start.9 = (bf16[32,128]{1,0:T(8,128)(2,1)S(1)}, bf16[32,128]{1,0:T(8,128)(2,1)S(1)}, u32[]{:S(2)}, u32[]{:S(2)}) collective-permute-start(bf16[32,128]{1,0:T(8,128)(2,1)S(1)} %slice.1287), channel_id=1, source_target_pairs={{0,32},{32,64},{64,96},{96,128},{128,160},{160,192},{192,224},{224... | collective-permute-start | bytes 24584 | tf_op jit(solution)/shard_map/ppermute | solution.py:19
  23.0 9.6 %collective-permute-start.5 = (bf16[128,128]{1,0:T(8,128)(2,1)}, bf16[128,128]{1,0:T(8,128)(2,1)S(1)}, u32[]{:S(2)}, u32[]{:S(2)}) collective-permute-start(bf16[128,128]{1,0:T(8,128)(2,1)} %param.12), channel_id=1, source_target_pairs={{0,128},{32,160},{64,192},{96,224},{128,256},{160,288},{192,320},{... | collective-permute-start | bytes 98312 | tf_op jit(solution)/shard_map/ppermute | solution.py:19
  25.1 7.6 %collective-permute-start.6 = (bf16[128,128]{1,0:T(8,128)(2,1)}, bf16[128,128]{1,0:T(8,128)(2,1)S(1)}, u32[]{:S(2)}, u32[]{:S(2)}) collective-permute-start(bf16[128,128]{1,0:T(8,128)(2,1)} %param.12), channel_id=1, source_target_pairs={{0,96},{32,128},{64,160},{96,192},{128,224},{160,256},{192,288},{2... | collective-permute-start | bytes 98312 | tf_op jit(solution)/shard_map/ppermute | solution.py:19
  26.4 7.7 %collective-permute-start.7 = (bf16[128,128]{1,0:T(8,128)(2,1)}, bf16[128,128]{1,0:T(8,128)(2,1)S(1)}, u32[]{:S(2)}, u32[]{:S(2)}) collective-permute-start(bf16[128,128]{1,0:T(8,128)(2,1)} %param.12), channel_id=1, source_target_pairs={{0,64},{32,96},{64,128},{96,160},{128,192},{160,224},{192,256},{22... | collective-permute-start | bytes 98312 | tf_op jit(solution)/shard_map/ppermute | solution.py:19
  27.7 6.4 %collective-permute-start.8 = (bf16[128,128]{1,0:T(8,128)(2,1)}, bf16[128,128]{1,0:T(8,128)(2,1)S(1)}, u32[]{:S(2)}, u32[]{:S(2)}) collective-permute-start(bf16[128,128]{1,0:T(8,128)(2,1)} %param.12), channel_id=1, source_target_pairs={{0,32},{32,64},{64,96},{96,128},{128,160},{160,192},{192,224},{224... | collective-permute-start | bytes 98312 | tf_op jit(solution)/shard_map/ppermute | solution.py:19
  76.6 369.7 %copy-start = (f32[4,8192]{1,0:T(4,128)S(1)}, f32[4,8192]{1,0:T(4,128)}, u32[]{:S(2)}) copy-start(f32[4,8192]{1,0:T(4,128)} %param.16) | copy-start | bytes 393220
Sparse Core Ops, SparseCore 0:
  15.1 52.4 all-gather.1
  81.7 364.5 all-reduce.2
where the time goes:
time: 456 us; the launch traced here: 455 us
  waiting for transfers between devices  370 us (81%)
  matrix products  18.2 us (4%)
  starting transfers between devices  15.4 us (3%)
  local copies, waits for them, and re-layouts  14.7 us (3%)
  between operations  14.2 us (3%)
  other arithmetic  13.5 us (3%)
  loops' own time  8.55 us (2%)
    unnamed x3, waiting for transfers between devices  363 us
    ppermute x10, starting transfers between devices, shifted(): lax.ppermute(value, axis, [(source, source + steps) for source in range(l...  15.4 us
  transfers between devices with their start and end apart: 12, of which 6 were waited for; matrix products, arithmetic and copies ran while one was open for 9% of the time, Pallas kernels for 0%

commit v1 on v0

v1 whole, which is shorter than its diff:
```python
import functools
import math

import jax
import jax.numpy as jnp
from jax import lax
from jax.experimental import pallas as pl
from jax.experimental.pallas import tpu as pltpu
from jax.sharding import PartitionSpec as P

DH = 128
W1 = 512
W2 = 32
TOK = 128
HL = 2
KSPAN = W1 + TOK
NX = 4
NZ = 8
NY = 4
NC = 8
BIG = -1e30
MESH = pl.DeviceIdType.MESH
F32 = jnp.float32
BF16 = jnp.bfloat16
SUB = 8


def kernel(
    q_ref, k_ref, v_ref, pk_ref, pv_ref, fkrow_ref, fks_ref, w_ref, out_ref,
    rhs, vaug, pkc, pvc, pkf, pvf, qf, lhs, prob, att, abuf, wf,
    rsend, rown, rrecv, ffin, fsend, frecv,
    hs, hr, w1s, w1r, w2s, w2r, w3s, w3r, a_s, a_r, rs_s, rs_r, f_s, f_r,
):
    s = lax.axis_index("seq")
    h = lax.axis_index("head")
    z = h // NY
    yh = h % NY
    core = s % 2
    c = s // 2
    x = c % NX
    yl = c // NX
    base = s * TOK

    def dev(seq, head):
        return {"seq": seq, "head": head}

    def rcopy(src, dst, ssem, rsem, seq, head):
        return pltpu.make_async_remote_copy(
            src_ref=src, dst_ref=dst, send_sem=ssem, recv_sem=rsem,
            device_id=dev(seq, head), device_id_type=MESH,
        )

    bar = pltpu.get_barrier_semaphore()
    count = 0
    for k in range(1, 16):
        pl.semaphore_signal(bar, inc=1, device_id=dev((s + k) % 16, h), device_id_type=MESH)
        count += 1
    for k in range(1, NZ):
        for dc in range(2):
            pl.semaphore_signal(
                bar, inc=1, device_id=dev(c * 2 + (core + dc) % 2, ((z + k) % NZ) * NY + yh),
                device_id_type=MESH)
            count += 1
    for k in range(1, NY):
        pl.semaphore_signal(bar, inc=1, device_id=dev(s, z * NY + (yh + k) % NY), device_id_type=MESH)
        count += 1
    pl.semaphore_wait(bar, count)

    def halo(o):
        rows = pl.ds((4 - o) * TOK, TOK)
        res = [
            rcopy(k_ref, rhs.at[rows, pl.ds(0, DH)], hs.at[o, 0], hr.at[o, 0], (s + o) % 16, h),
            rcopy(v_ref, vaug.at[rows, pl.ds(0, DH)], hs.at[o, 1], hr.at[o, 1], (s + o) % 16, h),
        ]
        if o == 1:
            tail = pl.ds(TOK - W2, W2)
            head = pl.ds(0, W2)
            res.append(rcopy(pk_ref.at[tail], pkc.at[head], hs.at[0, 0], hr.at[0, 0], (s + 1) % 16, h))
            res.append(rcopy(pv_ref.at[tail], pvc.at[head], hs.at[0, 1], hr.at[0, 1], (s + 1) % 16, h))
        return res

    for o in range(1, 5):
        @pl.when(s + o < 16)
        def _():
            for cp in halo(o):
                cp.start()

    ki = z % 2
    wi = z // 2

    def w1_copy(q):
        src = w_ref.at[:, pl.ds(q * 128, 128)]
        dst = wf.at[ki, c, wi]
        return src, dst, 4 * core + q

    for q in range(4):
        src, dst, zd = w1_copy(q)
        mine = (zd == z) & (ki == core)

        @pl.when(mine)
        def _():
            pltpu.make_async_copy(src, dst, w1r.at[wi]).start()

        @pl.when(jnp.logical_not(mine))
        def _():
            rcopy(src, dst, w1s.at[q], w1r.at[wi], c * 2 + ki, zd * NY + yh).start()

    rhs[pl.ds(W1, TOK), pl.ds(0, DH)] = k_ref[...]
    vaug[pl.ds(W1, TOK), pl.ds(0, DH)] = v_ref[...]
    vaug[:, pl.ds(DH, DH)] = jnp.ones((KSPAN, DH), BF16)
    for hd in range(HL):
        qf[hd] = q_ref[:, hd * DH:(hd + 1) * DH].astype(F32)
    pkf[pl.ds(W2, TOK), :] = pk_ref[...].astype(F32)
    pvf[pl.ds(W2, TOK), :] = pv_ref[...].astype(F32)
    for o in range(1, 5):
        @pl.when(s < o)
        def _():
            rhs[pl.ds((4 - o) * TOK, TOK), pl.ds(0, DH)] = jnp.zeros((TOK, DH), BF16)
            vaug[pl.ds((4 - o) * TOK, TOK), pl.ds(0, DH)] = jnp.zeros((TOK, DH), BF16)
            if o == 1:
                pkc[...] = jnp.zeros((W2, DH), BF16)
                pvc[...] = jnp.zeros((W2, DH), BF16)

    for o in range(1, 5):
        @pl.when(s >= o)
        def _():
            for cp in halo(o):
                cp.wait_recv()

    pkf[pl.ds(0, W2), :] = pkc[...].astype(F32)
    pvf[pl.ds(0, W2), :] = pvc[...].astype(F32)

    scale = math.log2(math.e) / math.sqrt(DH)
    lane = lax.broadcasted_iota(jnp.int32, (W2, DH), 1)
    orow = lax.broadcasted_iota(jnp.int32, (W2, DH), 0)

    def a_copy(n, kz):
        rows = pl.ds(n * 32, 32)
        return rcopy(
            abuf.at[z, rows], abuf.at[z, rows], a_s.at[n, kz], a_r.at[n, kz],
            s, ((z + kz) % NZ) * NY + yh)

    def attend(n):
        y = (yh + 1 + n) % NY
        tstar = 4 * ((y + 1) % NY)
        u = lax.broadcasted_iota(jnp.int32, (KSPAN, DH), 0)
        t = lax.broadcasted_iota(jnp.int32, (KSPAN, DH), 1)
        low = jnp.maximum(t + 1, fkrow_ref[...] - base + W1)
        ok = (u >= low) & (u <= t + W1) & (t != tstar)
        rhs[:, pl.ds(DH, DH)] = jnp.where(ok, 0.0, BIG).astype(BF16)

        def sub(i, carry):
            for j in range(SUB):
                tok = 16 * (2 * i + j // 4) + 4 * y + j % 4
                win = pkf[pl.ds(tok + 1, W2), :]
                bad = fks_ref[tok] - (base + tok) + (W2 - 1)
                hot = jnp.where((lane == tok) | ((lane == tstar) & (orow < bad)), 1.0, 0.0).astype(BF16)
                for hd in range(HL):
                    row = (j * HL + hd) * W2
                    qrow = qf[hd, pl.ds(tok, 1), :]
                    lhs[pl.ds(row, W2), pl.ds(0, DH)] = (win * qrow).astype(BF16)
                    lhs[pl.ds(row, W2), pl.ds(DH, DH)] = hot
            sc = lax.dot_general(
                lhs[...], rhs[...], (((1,), (1,)), ((), ())), preferred_element_type=F32)
            for g in range(SUB * HL):
                part = sc[g * W2:(g + 1) * W2]
                top = part[:, 0:128]
                for b in range(1, 5):
                    top = jnp.maximum(top, part[:, b * 128:(b + 1) * 128])
                top = jnp.maximum(jnp.maximum(top[0:8], top[8:16]), jnp.maximum(top[16:24], top[24:32]))
                top = jnp.max(jnp.max(top, axis=0, keepdims=True), axis=1, keepdims=True)
                prob[pl.ds(g * W2, W2), :] = jnp.exp2((part - top) * scale).astype(BF16)
            car = jnp.dot(prob[...], vaug[...], preferred_element_type=F32)
            for j in range(SUB):
                tok = 16 * (2 * i + j // 4) + 4 * y + j % 4
                win = pvf[pl.ds(tok + 1, W2), :]
                for hd in range(HL):
                    row = (j * HL + hd) * W2
                    num = car[row:row + W2, 0:DH] * win
                    den = car[row:row + W2, DH:2 * DH]
                    num = (num[0:8] + num[8:16]) + (num[16:24] + num[24:32])
                    den = (den[0:8] + den[8:16]) + (den[16:24] + den[24:32])
                    num = jnp.sum(num, axis=0, keepdims=True)
                    den = jnp.sum(den, axis=0, keepdims=True)
                    att[hd, pl.ds(i * SUB + j, 1), :] = num / den
            return carry

        lax.fori_loop(0, 32 // SUB, sub, 0)
        for hd in range(HL):
            abuf[z, pl.ds(n * 32, 32), pl.ds(hd * DH, DH)] = att[hd].astype(BF16)
        for kz in range(1, NZ):
            a_copy(n, kz).start()

    def chip(d):
        return ((yl + d // NX) % 2) * NX + (x + d % NX) % NX

    def chip_from(d):
        return ((yl + d // NX) % 2) * NX + (x + NX - d % NX) % NX

    def w2_copy(d, i):
        return rcopy(wf.at[core, c, i], wf.at[core, c, i], w2s.at[d, i], w2r.at[d, i], chip(d) * 2 + core, h)

    def w3_copy(d):
        blk = wf.at[core, chip_from(d)]
        return rcopy(blk, blk, w3s.at[d], w3r.at[d], c * 2 + (core + 1) % 2, h)

    attend(0)
    for i in range(4):
        pltpu.make_async_copy(wf.at[core, c, i], wf.at[core, c, i], w1r.at[i]).wait()
        for d in range(1, NC):
            w2_copy(d, i).start()
    w3_copy(0).start()
    for n in range(1, 4):
        attend(n)

    for n in range(4):
        for kz in range(1, NZ):
            a_copy(n, kz).wait_recv()

    def rs_copy(n, pair):
        return rcopy(
            rsend.at[n, pair], rrecv.at[n, pair], rs_s.at[n, pair], rs_r.at[n, pair],
            s, z * NY + (yh + 1 + n) % NY)

    order = (0, 1, 3, 4, 2, 5, 7, 6)
    for pair in range(4):
        ds = order[2 * pair:2 * pair + 2]
        for d in ds:
            if d > 0:
                for i in range(4):
                    w2_copy(d, i).wait_recv()
                w3_copy(d).start()
        for d in ds:
            w3_copy(d).wait_recv()
        acc = None
        for zz in range(NZ):
            rhs_w = jnp.concatenate([wf[zz % 2, chip_from(d), zz // 2] for d in ds], axis=1)
            term = jnp.dot(abuf[zz], rhs_w, preferred_element_type=F32)
            acc = term if acc is None else acc + term
        for n in range(3):
            rsend[n, pair] = acc[n * 32:(n + 1) * 32].astype(BF16)
            rs_copy(n, pair).start()
        rown[pair] = acc[96:128]

    for pair in range(4):
        total = rown[pair]
        for n in range(3):
            rs_copy(n, pair).wait_recv()
            total = total + rrecv[n, pair].astype(F32)
        for e in range(2):
            for zz in range(NZ):
                ffin[zz, pl.ds((2 * pair + e) * 4, 4), :] = total[zz * 4:zz * 4 + 4, e * 128:(e + 1) * 128]
    fsend[...] = ffin[...].astype(BF16)

    def f_copy(kz):
        return rcopy(
            fsend.at[(z + kz) % NZ], frecv.at[kz], f_s.at[kz], f_r.at[kz], s, ((z + kz) % NZ) * NY + yh)

    for kz in range(1, NZ):
        f_copy(kz).start()

    def place(val, zs):
        for e in range(NC):
            col = chip_from(order[e]) * (NZ * 128) + zs * 128
            out_ref[:, pl.ds(pl.multiple_of(col, 128), 128)] = val[e * 4:e * 4 + 4]

    place(ffin[z], z)
    for kz in range(1, NZ):
        f_copy(kz).wait_recv()
        place(frecv[kz].astype(F32), (z + NZ - kz) % NZ)

    for o in range(1, 5):
        @pl.when(s + o < 16)
        def _():
            for cp in halo(o):
                cp.wait_send()
    for q in range(4):
        src, dst, zd = w1_copy(q)

        @pl.when(jnp.logical_not((zd == z) & (ki == core)))
        def _():
            rcopy(src, dst, w1s.at[q], w1r.at[wi], c * 2 + ki, zd * NY + yh).wait_send()
    for d in range(1, NC):
        for i in range(4):
            w2_copy(d, i).wait_send()
    for d in range(NC):
        w3_copy(d).wait_send()
    for n in range(4):
        for kz in range(1, NZ):
            a_copy(n, kz).wait_send()
    for n in range(3):
        for pair in range(4):
            rs_copy(n, pair).wait_send()
    for kz in range(1, NZ):
        f_copy(kz).wait_send()


def local(queries, key_rows, value_rows, pair_keys, pair_values, first_key, residual, out_weight):
    vm = pl.BlockSpec(memory_space=pltpu.VMEM)
    dma = pltpu.SemaphoreType.DMA
    summed = pl.pallas_call(
        kernel,
        out_shape=jax.ShapeDtypeStruct((4, 8192), F32),
        in_specs=[vm, vm, vm, vm, vm, vm, pl.BlockSpec(memory_space=pltpu.SMEM),
                  pl.BlockSpec(memory_space=pl.ANY)],
        out_specs=vm,
        scratch_shapes=[
            pltpu.VMEM((KSPAN, 2 * DH), BF16),
            pltpu.VMEM((KSPAN, 2 * DH), BF16),
            pltpu.VMEM((W2, DH), BF16),
            pltpu.VMEM((W2, DH), BF16),
            pltpu.VMEM((W2 + TOK, DH), F32),
            pltpu.VMEM((W2 + TOK, DH), F32),
            pltpu.VMEM((HL, TOK, DH), F32),
            pltpu.VMEM((SUB * HL * W2, 2 * DH), BF16),
            pltpu.VMEM((SUB * HL * W2, KSPAN), BF16),
            pltpu.VMEM((HL, 32, DH), F32),
            pltpu.VMEM((NZ, TOK, HL * DH), BF16),
            pltpu.VMEM((2, NC, 4, HL * DH, 128), BF16),
            pltpu.VMEM((3, 4, 32, 256), BF16),
            pltpu.VMEM((4, 32, 256), F32),
            pltpu.VMEM((3, 4, 32, 256), BF16),
            pltpu.VMEM((NZ, 32, 128), F32),
            pltpu.VMEM((NZ, 32, 128), BF16),
            pltpu.VMEM((NZ, 32, 128), BF16),
            dma((5, 2)), dma((5, 2)),
            dma((4,)), dma((4,)),
            dma((NC, 4)), dma((NC, 4)),
            dma((NC,)), dma((NC,)),
            dma((4, NZ)), dma((4, NZ)),
            dma((3, 4)), dma((3, 4)),
            dma((NZ,)), dma((NZ,)),
        ],
        compiler_params=pltpu.CompilerParams(collective_id=0, has_side_effects=True),
        name="layer",
    )(queries, key_rows, value_rows, pair_keys, pair_values, first_key.reshape(1, TOK), first_key, out_weight)
    return residual + summed


def solution(mesh):
    placed = (
        P("seq", "head"),
        P("seq", None),
        P("seq", None),
        P("seq", None),
        P("seq", None),
        P("seq"),
        P(("seq", "head"), None),
        P("head", "seq"),
    )
    return jax.shard_map(
        local, mesh=mesh, in_specs=placed, out_specs=P(("seq", "head"), None), check_vma=False
    )
```

time: 456 us -> 72.2 us (0.16)
  the two profiles are of different devices: /device:TPU:14 before, /device:TPU:1 now
where the time goes in v1:
time: 72.2 us; the launch traced here: 72 us
  Pallas kernels  70.4 us (98%)
  other arithmetic  1.6 us (2%)
    pallas_call x1, Pallas kernels, local(): pl.pallas_call(kernel, out_shape=jax.ShapeDtypeStruct((4, 8192), F32), in...  70.4 us
    add x1, other arithmetic, local(): return residual + summed  1.6 us

profile of v1, /device:TPU:1, one launch (start us, length us, event | category | flops | bytes accessed | tf_op | source)
XLA Modules:
  0.0 72.0 jit_solution(16292469546125138394)
XLA Ops:
  0.0 0.0 copy-start
  0.0 70.4 %layer.1 = f32[4,8192]{1,0:T(4,128)} custom-call(bf16[128,256]{1,0:T(8,128)(2,1)} %q_ref.1, bf16[128,128]{1,0:T(8,128)(2,1)} %k_ref.1, bf16[128,128]{1,0:T(8,128)(2,1)} %v_ref.1, bf16[128,128]{1,0:T(8,128)(2,1)} %pk_ref.1, bf16[128,128]{1,0:T(8,128)(2,1)} %pv_ref.1, s32[1,128]{1,0:T(1,128)} %bitcast.1, s32[128]{0:T(128)} %fks_ref.1, bf16[256,512]{1,0:T(8,128)(2,1)} %w_ref.1), custom_call_target="tpu_custom_call" | custom-call | tf_op jit(solution)/shard_map/layer/pallas_call | solution.py:301
  70.4 0.0 copy-done
  70.4 1.6 %add.3 = f32[4,8192]{1,0:T(4,128)} add(f32[4,8192]{1,0:T(4,128)S(1)} %copy-done, f32[4,8192]{1,0:T(4,128)} %layer.1) | non-fusion elementwise | flops 32768 | bytes 393216 | tf_op jit(solution)/shard_map/add | solution.py:337
Async XLA Ops:
  0.0 70.4 %copy-start = (f32[4,8192]{1,0:T(4,128)S(1)}, f32[4,8192]{1,0:T(4,128)}, u32[]{:S(2)}) copy-start(f32[4,8192]{1,0:T(4,128)} %param.14) | copy-start | bytes 393220

commit v2 on v1

--- a/solution.py
+++ b/solution.py
@@ -185,33 +185,59 @@
                     att[hd, pl.ds(i * SUB + j, 1), :] = num / den
             return carry
 
-        lax.fori_loop(0, 32 // SUB, sub, 0)
+        lax.fori_loop(0, 32 // SUB, sub, 0, unroll=True)
         for hd in range(HL):
             abuf[z, pl.ds(n * 32, 32), pl.ds(hd * DH, DH)] = att[hd].astype(BF16)
         for kz in range(1, NZ):
             a_copy(n, kz).start()
 
-    def chip(d):
-        return ((yl + d // NX) % 2) * NX + (x + d % NX) % NX
-
     def chip_from(d):
         return ((yl + d // NX) % 2) * NX + (x + NX - d % NX) % NX
 
-    def w2_copy(d, i):
-        return rcopy(wf.at[core, c, i], wf.at[core, c, i], w2s.at[d, i], w2r.at[d, i], chip(d) * 2 + core, h)
+    def seq_at(dx, dy):
+        return (((yl + dy) % 2) * NX + (x + NX + dx) % NX) * 2 + core
+
+    def w2_send(d, i, to):
+        dx, dy = to
+        e = ((d // NX + dy) % 2) * NX + (d % NX + dx) % NX
+        blk = wf.at[core, chip_from(d), i]
+        return rcopy(blk, blk, w2s.at[e, i], w2r.at[e, i], seq_at(dx, dy), h)
+
+    def w2_wait(d, i):
+        blk = wf.at[core, chip_from(d), i]
+        rcopy(blk, blk, w2s.at[d, i], w2r.at[d, i], seq_at(1, 0), h).wait_recv()
 
     def w3_copy(d):
         blk = wf.at[core, chip_from(d)]
         return rcopy(blk, blk, w3s.at[d], w3r.at[d], c * 2 + (core + 1) % 2, h)
 
-    attend(0)
+    right, left, across = (1, 0), (-1, 0), (0, 1)
+    relays = (
+        (((1, 0), (right,)), ((4, 0), (right, left))),
+        (((1, 1), (across,)), ((3, 1), (left,)), ((4, 1), (left,))),
+        (((1, 2), (across,)), ((3, 2), (left,)), ((4, 2), (left,)),
+         ((1, 3), (across,)), ((3, 3), (left, across)), ((7, 0), (left,))),
+        (((7, 1), (left,)), ((2, 2), (across,)), ((2, 3), (across,))),
+    )
+    seen = set()
+
+    def relay(step):
+        for (d, i), targets in relays[step]:
+            w2_wait(d, i)
+            seen.add((d, i))
+            for to in targets:
+                w2_send(d, i, to).start()
+
     for i in range(4):
         pltpu.make_async_copy(wf.at[core, c, i], wf.at[core, c, i], w1r.at[i]).wait()
-        for d in range(1, NC):
-            w2_copy(d, i).start()
+        for to in (right, left, across):
+            w2_send(0, i, to).start()
     w3_copy(0).start()
-    for n in range(1, 4):
+    for n in range(4):
         attend(n)
+        relay(n)
+        if n == 2:
+            w3_copy(1).start()
 
     for n in range(4):
         for kz in range(1, NZ):
@@ -222,13 +248,14 @@
             rsend.at[n, pair], rrecv.at[n, pair], rs_s.at[n, pair], rs_r.at[n, pair],
             s, z * NY + (yh + 1 + n) % NY)
 
-    order = (0, 1, 3, 4, 2, 5, 7, 6)
+    order = (0, 1, 3, 4, 2, 7, 5, 6)
     for pair in range(4):
         ds = order[2 * pair:2 * pair + 2]
         for d in ds:
-            if d > 0:
+            if d > 1:
                 for i in range(4):
-                    w2_copy(d, i).wait_recv()
+                    if (d, i) not in seen:
+                        w2_wait(d, i)
                 w3_copy(d).start()
         for d in ds:
             w3_copy(d).wait_recv()
@@ -280,9 +307,13 @@
         @pl.when(jnp.logical_not((zd == z) & (ki == core)))
         def _():
             rcopy(src, dst, w1s.at[q], w1r.at[wi], c * 2 + ki, zd * NY + yh).wait_send()
-    for d in range(1, NC):
-        for i in range(4):
-            w2_copy(d, i).wait_send()
+    for i in range(4):
+        for to in (right, left, across):
+            w2_send(0, i, to).wait_send()
+    for step in relays:
+        for (d, i), targets in step:
+            for to in targets:
+                w2_send(d, i, to).wait_send()
     for d in range(NC):
         w3_copy(d).wait_send()
     for n in range(4):

time: 72.2 us -> 62.3 us (0.86)
  Pallas kernels: 70.4 us -> 60.3 us
    pallas_call x1, Pallas kernels: 70.4 us -> 60.3 us  [local(): pl.pallas_call(kernel, out_shape=jax.ShapeDtypeStruct((4, 8192), F32), in...]
where the time goes in v2:
time: 62.3 us; the launch traced here: 61.9 us
  Pallas kernels  60.3 us (97%)
  other arithmetic  1.6 us (3%)
    pallas_call x1, Pallas kernels, local(): pl.pallas_call(kernel, out_shape=jax.ShapeDtypeStruct((4, 8192), F32), in...  60.3 us
    add x1, other arithmetic, local(): return residual + summed  1.6 us

profile of v2, /device:TPU:1, one launch (start us, length us, event | category | flops | bytes accessed | tf_op | source)
XLA Modules:
  0.0 61.9 jit_solution(14912563235411204698)
XLA Ops:
  0.0 0.0 copy-start
  0.0 60.3 %layer.1 = f32[4,8192]{1,0:T(4,128)} custom-call(bf16[128,256]{1,0:T(8,128)(2,1)} %q_ref.1, bf16[128,128]{1,0:T(8,128)(2,1)} %k_ref.1, bf16[128,128]{1,0:T(8,128)(2,1)} %v_ref.1, bf16[128,128]{1,0:T(8,128)(2,1)} %pk_ref.1, bf16[128,128]{1,0:T(8,128)(2,1)} %pv_ref.1, s32[1,128]{1,0:T(1,128)} %bitcast.1, s32[128]{0:T(128)} %fks_ref.1, bf16[256,512]{1,0:T(8,128)(2,1)} %w_ref.1), custom_call_target="tpu_custom_call" | custom-call | tf_op jit(solution)/shard_map/layer/pallas_call | solution.py:332
  60.3 0.0 copy-done
  60.3 1.6 %add.3 = f32[4,8192]{1,0:T(4,128)} add(f32[4,8192]{1,0:T(4,128)S(1)} %copy-done, f32[4,8192]{1,0:T(4,128)} %layer.1) | non-fusion elementwise | flops 32768 | bytes 393216 | tf_op jit(solution)/shard_map/add | solution.py:368
Async XLA Ops:
  0.0 60.3 %copy-start = (f32[4,8192]{1,0:T(4,128)S(1)}, f32[4,8192]{1,0:T(4,128)}, u32[]{:S(2)}) copy-start(f32[4,8192]{1,0:T(4,128)} %param.14) | copy-start | bytes 393220

commit v3 on v1

--- a/solution.py
+++ b/solution.py
@@ -28,8 +28,8 @@
 def kernel(
     q_ref, k_ref, v_ref, pk_ref, pv_ref, fkrow_ref, fks_ref, w_ref, out_ref,
     rhs, vaug, pkc, pvc, pkf, pvf, qf, lhs, prob, att, abuf, wf,
-    rsend, rown, rrecv, ffin, fsend, frecv,
-    hs, hr, w1s, w1r, w2s, w2r, w3s, w3r, a_s, a_r, rs_s, rs_r, f_s, f_r,
+    ffin, fsend, frecv,
+    hs, hr, w1s, w1r, w2s, w2r, w3s, w3r, a_s, a_r, f_s, f_r,
 ):
     s = lax.axis_index("seq")
     h = lax.axis_index("head")
@@ -85,16 +85,18 @@
             for cp in halo(o):
                 cp.start()
 
+    near = (0, 1, 3, 2)
     ki = z % 2
     wi = z // 2
 
-    def w1_copy(q):
-        src = w_ref.at[:, pl.ds(q * 128, 128)]
+    def w1_copy(k):
+        q = (z + near[k]) % 4
+        src = w_ref.at[:, pl.ds(pl.multiple_of(q * 128, 128), 128)]
         dst = wf.at[ki, c, wi]
         return src, dst, 4 * core + q
 
-    for q in range(4):
-        src, dst, zd = w1_copy(q)
+    for k in range(4):
+        src, dst, zd = w1_copy(k)
         mine = (zd == z) & (ki == core)
 
         @pl.when(mine)
@@ -103,7 +105,52 @@
 
         @pl.when(jnp.logical_not(mine))
         def _():
-            rcopy(src, dst, w1s.at[q], w1r.at[wi], c * 2 + ki, zd * NY + yh).start()
+            rcopy(src, dst, w1s.at[k], w1r.at[wi], c * 2 + ki, zd * NY + yh).start()
+
+    def chip_from(d):
+        return ((yl + d // NX) % 2) * NX + (x + NX - d % NX) % NX
+
+    def seq_at(dx, dy):
+        return (((yl + dy) % 2) * NX + (x + NX + dx) % NX) * 2 + core
+
+    def w2_send(d, i, to):
+        dx, dy = to
+        e = ((d // NX + dy) % 2) * NX + (d % NX + dx) % NX
+        blk = wf.at[core, chip_from(d), (wi + near[i]) % 4]
+        return rcopy(blk, blk, w2s.at[e, i], w2r.at[e, i], seq_at(dx, dy), h)
+
+    def w2_wait(d, i):
+        blk = wf.at[core, chip_from(d), (wi + near[i]) % 4]
+        rcopy(blk, blk, w2s.at[d, i], w2r.at[d, i], seq_at(1, 0), h).wait_recv()
+
+    def w3_copy(d, i):
+        blk = wf.at[core, chip_from(d), (wi + near[i]) % 4]
+        return rcopy(blk, blk, w3s.at[d, i], w3r.at[d, i], c * 2 + (core + 1) % 2, h)
+
+    right, left, across = (1, 0), (-1, 0), (0, 1)
+    relays = (
+        (((1, 0), (right,)), ((4, 0), (right, left))),
+        (((1, 1), (across,)), ((3, 1), (left,)), ((4, 1), (left,))),
+        (((1, 2), (across,)), ((3, 2), (left,)), ((4, 2), (left,)),
+         ((1, 3), (across,)), ((3, 3), (left, across)), ((7, 0), (left,))),
+        (((7, 1), (left,)), ((2, 2), (across,)), ((2, 3), (across,))),
+    )
+    seen = set()
+
+    def relay(step):
+        for (d, i), targets in relays[step]:
+            w2_wait(d, i)
+            seen.add((d, i))
+            for to in targets:
+                w2_send(d, i, to).start()
+            w3_copy(d, i).start()
+
+    def w2_first(k):
+        blk = wf.at[core, c, (wi + near[k]) % 4]
+        pltpu.make_async_copy(blk, blk, w1r.at[(wi + near[k]) % 4]).wait()
+        for to in (right, left, across):
+            w2_send(0, k, to).start()
+        w3_copy(0, k).start()
 
     rhs[pl.ds(W1, TOK), pl.ds(0, DH)] = k_ref[...]
     vaug[pl.ds(W1, TOK), pl.ds(0, DH)] = v_ref[...]
@@ -121,11 +168,14 @@
                 pkc[...] = jnp.zeros((W2, DH), BF16)
                 pvc[...] = jnp.zeros((W2, DH), BF16)
 
+    w2_first(0)
+    w2_first(1)
     for o in range(1, 5):
         @pl.when(s >= o)
         def _():
             for cp in halo(o):
                 cp.wait_recv()
+    w2_first(2)
 
     pkf[pl.ds(0, W2), :] = pkc[...].astype(F32)
     pvf[pl.ds(0, W2), :] = pvc[...].astype(F32)
@@ -185,114 +235,119 @@
                     att[hd, pl.ds(i * SUB + j, 1), :] = num / den
             return carry
 
-        lax.fori_loop(0, 32 // SUB, sub, 0)
+        lax.fori_loop(0, 32 // SUB, sub, 0, unroll=True)
         for hd in range(HL):
             abuf[z, pl.ds(n * 32, 32), pl.ds(hd * DH, DH)] = att[hd].astype(BF16)
-        for kz in range(1, NZ):
+        for kz in (4, 3, 5, 2, 6, 1, 7):
             a_copy(n, kz).start()
 
-    def chip(d):
-        return ((yl + d // NX) % 2) * NX + (x + d % NX) % NX
-
-    def chip_from(d):
-        return ((yl + d // NX) % 2) * NX + (x + NX - d % NX) % NX
-
-    def w2_copy(d, i):
-        return rcopy(wf.at[core, c, i], wf.at[core, c, i], w2s.at[d, i], w2r.at[d, i], chip(d) * 2 + core, h)
-
-    def w3_copy(d):
-        blk = wf.at[core, chip_from(d)]
-        return rcopy(blk, blk, w3s.at[d], w3r.at[d], c * 2 + (core + 1) % 2, h)
-
-    attend(0)
-    for i in range(4):
-        pltpu.make_async_copy(wf.at[core, c, i], wf.at[core, c, i], w1r.at[i]).wait()
-        for d in range(1, NC):
-            w2_copy(d, i).start()
-    w3_copy(0).start()
-    for n in range(1, 4):
+    for n in range(4):
         attend(n)
+        if n == 0:
+            w2_first(3)
+        relay(n)
 
     for n in range(4):
         for kz in range(1, NZ):
             a_copy(n, kz).wait_recv()
 
-    def rs_copy(n, pair):
+    groups = ((0, 2), (2, 3), (3, 4))
+
+    def f_copy(g, n, kz):
+        lo, hi = groups[g]
+        part = pl.ds(lo, hi - lo)
         return rcopy(
-            rsend.at[n, pair], rrecv.at[n, pair], rs_s.at[n, pair], rs_r.at[n, pair],
-            s, z * NY + (yh + 1 + n) % NY)
-
-    order = (0, 1, 3, 4, 2, 5, 7, 6)
-    for pair in range(4):
+            fsend.at[n, (z + kz) % NZ, part], frecv.at[n, kz, part],
+            f_s.at[g, n, kz], f_r.at[g, n, kz],
+            s, ((z + kz) % NZ) * NY + (yh + 1 + n) % NY)
+
+    def hops(peer):
+        n, kz = peer
+        return min(kz, NZ - kz) + (0, 2, 4, 2)[(n + 1) % NY]
+
+    peers = tuple(sorted(
+        ((n, kz) for n in range(4) for kz in range(NZ) if (n, kz) != (3, 0)), key=hops, reverse=True))
+
+    order = (0, 1, 3, 4, 2, 7, 5, 6)
+
+    def columns(pair):
         ds = order[2 * pair:2 * pair + 2]
         for d in ds:
             if d > 0:
                 for i in range(4):
-                    w2_copy(d, i).wait_recv()
-                w3_copy(d).start()
+                    if (d, i) not in seen:
+                        w2_wait(d, i)
+                        w3_copy(d, i).start()
         for d in ds:
-            w3_copy(d).wait_recv()
+            for i in range(4):
+                w3_copy(d, i).wait_recv()
         acc = None
         for zz in range(NZ):
             rhs_w = jnp.concatenate([wf[zz % 2, chip_from(d), zz // 2] for d in ds], axis=1)
             term = jnp.dot(abuf[zz], rhs_w, preferred_element_type=F32)
             acc = term if acc is None else acc + term
-        for n in range(3):
-            rsend[n, pair] = acc[n * 32:(n + 1) * 32].astype(BF16)
-            rs_copy(n, pair).start()
-        rown[pair] = acc[96:128]
-
-    for pair in range(4):
-        total = rown[pair]
-        for n in range(3):
-            rs_copy(n, pair).wait_recv()
-            total = total + rrecv[n, pair].astype(F32)
-        for e in range(2):
-            for zz in range(NZ):
-                ffin[zz, pl.ds((2 * pair + e) * 4, 4), :] = total[zz * 4:zz * 4 + 4, e * 128:(e + 1) * 128]
-    fsend[...] = ffin[...].astype(BF16)
-
-    def f_copy(kz):
-        return rcopy(
-            fsend.at[(z + kz) % NZ], frecv.at[kz], f_s.at[kz], f_r.at[kz], s, ((z + kz) % NZ) * NY + yh)
-
-    for kz in range(1, NZ):
-        f_copy(kz).start()
-
-    def place(val, zs):
-        for e in range(NC):
-            col = chip_from(order[e]) * (NZ * 128) + zs * 128
-            out_ref[:, pl.ds(pl.multiple_of(col, 128), 128)] = val[e * 4:e * 4 + 4]
-
-    place(ffin[z], z)
-    for kz in range(1, NZ):
-        f_copy(kz).wait_recv()
-        place(frecv[kz].astype(F32), (z + NZ - kz) % NZ)
+        for n in range(4):
+            for e in range(2):
+                for zz in range(NZ):
+                    row = n * 32 + zz * 4
+                    ffin[n, zz, pair, pl.ds(e * 4, 4), :] = acc[row:row + 4, e * 128:(e + 1) * 128]
+
+    def push(g):
+        lo, hi = groups[g]
+        for n in range(4):
+            fsend[n, :, lo:hi] = ffin[n, :, lo:hi].astype(BF16)
+        for n, kz in peers:
+            f_copy(g, n, kz).start()
+
+    def place(g, kz):
+        lo, hi = groups[g]
+        total = ffin[3, z, lo:hi] if kz == 0 else None
+        for n in range(4):
+            if (n, kz) in peers:
+                f_copy(g, n, kz).wait_recv()
+                term = frecv[n, kz, lo:hi].astype(F32)
+                total = term if total is None else total + term
+        zs = (z + NZ - kz) % NZ
+        for pair in range(lo, hi):
+            for e in range(2):
+                col = chip_from(order[2 * pair + e]) * (NZ * 128) + zs * 128
+                out_ref[:, pl.ds(pl.multiple_of(col, 128), 128)] = total[pair - lo, e * 4:e * 4 + 4]
+
+    for g in range(3):
+        for pair in range(*groups[g]):
+            columns(pair)
+        push(g)
+    for g in range(3):
+        for kz in range(NZ):
+            place(g, kz)
 
     for o in range(1, 5):
         @pl.when(s + o < 16)
         def _():
             for cp in halo(o):
                 cp.wait_send()
-    for q in range(4):
-        src, dst, zd = w1_copy(q)
+    for k in range(4):
+        src, dst, zd = w1_copy(k)
 
         @pl.when(jnp.logical_not((zd == z) & (ki == core)))
         def _():
-            rcopy(src, dst, w1s.at[q], w1r.at[wi], c * 2 + ki, zd * NY + yh).wait_send()
-    for d in range(1, NC):
+            rcopy(src, dst, w1s.at[k], w1r.at[wi], c * 2 + ki, zd * NY + yh).wait_send()
+    for i in range(4):
+        for to in (right, left, across):
+            w2_send(0, i, to).wait_send()
+    for step in relays:
+        for (d, i), targets in step:
+            for to in targets:
+                w2_send(d, i, to).wait_send()
+    for d in range(NC):
         for i in range(4):
-            w2_copy(d, i).wait_send()
-    for d in range(NC):
-        w3_copy(d).wait_send()
+            w3_copy(d, i).wait_send()
     for n in range(4):
         for kz in range(1, NZ):
             a_copy(n, kz).wait_send()
-    for n in range(3):
-        for pair in range(4):
-            rs_copy(n, pair).wait_send()
-    for kz in range(1, NZ):
-        f_copy(kz).wait_send()
+    for g in range(3):
+        for n, kz in peers:
+            f_copy(g, n, kz).wait_send()
 
 
 def local(queries, key_rows, value_rows, pair_keys, pair_values, first_key, residual, out_weight):
@@ -317,19 +372,15 @@
             pltpu.VMEM((HL, 32, DH), F32),
             pltpu.VMEM((NZ, TOK, HL * DH), BF16),
             pltpu.VMEM((2, NC, 4, HL * DH, 128), BF16),
-            pltpu.VMEM((3, 4, 32, 256), BF16),
-            pltpu.VMEM((4, 32, 256), F32),
-            pltpu.VMEM((3, 4, 32, 256), BF16),
-            pltpu.VMEM((NZ, 32, 128), F32),
-            pltpu.VMEM((NZ, 32, 128), BF16),
-            pltpu.VMEM((NZ, 32, 128), BF16),
-            dma((5, 2)), dma((5, 2)),
+            pltpu.VMEM((4, NZ, 4, 8, 128), F32),
+            pltpu.VMEM((4, NZ, 4, 8, 128), BF16),
+            pltpu.VMEM((4, NZ, 4, 8, 128), BF16),
+            dma((8, 2)), dma((5, 2)),
             dma((4,)), dma((4,)),
             dma((NC, 4)), dma((NC, 4)),
-            dma((NC,)), dma((NC,)),
+            dma((NC, 4)), dma((NC, 4)),
             dma((4, NZ)), dma((4, NZ)),
-            dma((3, 4)), dma((3, 4)),
-            dma((NZ,)), dma((NZ,)),
+            dma((3, 4, NZ)), dma((3, 4, NZ)),
         ],
         compiler_params=pltpu.CompilerParams(collective_id=0, has_side_effects=True),
         name="layer",

time: 72.2 us -> 60.6 us (0.84); the launches traced: 72 us -> 59.6 us
  Pallas kernels: 70.4 us -> 58 us
    pallas_call x1, Pallas kernels: 70.4 us -> 58 us  [local(): pl.pallas_call(kernel, out_shape=jax.ShapeDtypeStruct((4, 8192), F32), in...]
where the time goes in v3:
time: 60.6 us; the launch traced here: 59.6 us
  Pallas kernels  58 us (96%)
  other arithmetic  1.6 us (3%)
    pallas_call x1, Pallas kernels, local(): pl.pallas_call(kernel, out_shape=jax.ShapeDtypeStruct((4, 8192), F32), in...  58 us
    add x1, other arithmetic, local(): return residual + summed  1.6 us

profile of v3, /device:TPU:1, one launch (start us, length us, event | category | flops | bytes accessed | tf_op | source)
XLA Modules:
  0.0 59.6 jit_solution(7310670189269190604)
XLA Ops:
  0.0 0.0 copy-start
  0.0 58.0 %layer.1 = f32[4,8192]{1,0:T(4,128)} custom-call(bf16[128,256]{1,0:T(8,128)(2,1)} %q_ref.1, bf16[128,128]{1,0:T(8,128)(2,1)} %k_ref.1, bf16[128,128]{1,0:T(8,128)(2,1)} %v_ref.1, bf16[128,128]{1,0:T(8,128)(2,1)} %pk_ref.1, bf16[128,128]{1,0:T(8,128)(2,1)} %pv_ref.1, s32[1,128]{1,0:T(1,128)} %bitcast.1, s32[128]{0:T(128)} %fks_ref.1, bf16[256,512]{1,0:T(8,128)(2,1)} %w_ref.1), custom_call_target="tpu_custom_call" | custom-call | tf_op jit(solution)/shard_map/layer/pallas_call | solution.py:356
  58.0 0.0 copy-done
  58.0 1.6 %add.3 = f32[4,8192]{1,0:T(4,128)} add(f32[4,8192]{1,0:T(4,128)S(1)} %copy-done, f32[4,8192]{1,0:T(4,128)} %layer.1) | non-fusion elementwise | flops 32768 | bytes 393216 | tf_op jit(solution)/shard_map/add | solution.py:388
Async XLA Ops:
  0.0 58.0 %copy-start = (f32[4,8192]{1,0:T(4,128)S(1)}, f32[4,8192]{1,0:T(4,128)}, u32[]{:S(2)}) copy-start(f32[4,8192]{1,0:T(4,128)} %param.14) | copy-start | bytes 393220

commit v4 on v3

--- a/solution.py
+++ b/solution.py
@@ -129,7 +129,7 @@
 
     right, left, across = (1, 0), (-1, 0), (0, 1)
     relays = (
-        (((1, 0), (right,)), ((4, 0), (right, left))),
+        (((3, 0), (left,)), ((4, 0), (right, left))),
         (((1, 1), (across,)), ((3, 1), (left,)), ((4, 1), (left,))),
         (((1, 2), (across,)), ((3, 2), (left,)), ((4, 2), (left,)),
          ((1, 3), (across,)), ((3, 3), (left, across)), ((7, 0), (left,))),

time: 60.6 us -> 62.1 us (1.025)
  the two profiles are of different devices: /device:TPU:1 before, /device:TPU:8 now
where the time goes in v4:
time: 62.1 us; the launch traced here: 61.9 us
  Pallas kernels  60.3 us (97%)
  other arithmetic  1.6 us (3%)
    pallas_call x1, Pallas kernels, local(): pl.pallas_call(kernel, out_shape=jax.ShapeDtypeStruct((4, 8192), F32), in...  60.3 us
    add x1, other arithmetic, local(): return residual + summed  1.6 us

profile of v4, /device:TPU:8, one launch (start us, length us, event | category | flops | bytes accessed | tf_op | source)
XLA Modules:
  0.0 61.9 jit_solution(11437187100296910852)
XLA Ops:
  0.0 0.0 copy-start
  0.0 60.3 %layer.1 = f32[4,8192]{1,0:T(4,128)} custom-call(bf16[128,256]{1,0:T(8,128)(2,1)} %q_ref.1, bf16[128,128]{1,0:T(8,128)(2,1)} %k_ref.1, bf16[128,128]{1,0:T(8,128)(2,1)} %v_ref.1, bf16[128,128]{1,0:T(8,128)(2,1)} %pk_ref.1, bf16[128,128]{1,0:T(8,128)(2,1)} %pv_ref.1, s32[1,128]{1,0:T(1,128)} %bitcast.1, s32[128]{0:T(128)} %fks_ref.1, bf16[256,512]{1,0:T(8,128)(2,1)} %w_ref.1), custom_call_target="tpu_custom_call" | custom-call | tf_op jit(solution)/shard_map/layer/pallas_call | solution.py:356
  60.3 0.0 copy-done
  60.3 1.6 %add.3 = f32[4,8192]{1,0:T(4,128)} add(f32[4,8192]{1,0:T(4,128)S(1)} %copy-done, f32[4,8192]{1,0:T(4,128)} %layer.1) | non-fusion elementwise | flops 32768 | bytes 393216 | tf_op jit(solution)/shard_map/add | solution.py:388
Async XLA Ops:
  0.0 60.3 %copy-start = (f32[4,8192]{1,0:T(4,128)S(1)}, f32[4,8192]{1,0:T(4,128)}, u32[]{:S(2)}) copy-start(f32[4,8192]{1,0:T(4,128)} %param.14) | copy-start | bytes 393220
